TPU v7x, 32 devices: a whole 2x2x4 slice. The times are simulated.
32 devices in a mesh: batch: 4 (over x, core), hidden: 4 (over z), solver: 2 (over y).
Axes of the slice: x: 2, y: 2, z: 4, core: 2. Of those that a mesh axis runs over, the one named last changes fastest.
Arguments:
- activations: bfloat16 [1024, 4096], P('batch', ('hidden', 'solver')), may hold values from -16 to 16, as said below
- cotangent: bfloat16 [8192, 1024], P(('hidden', 'solver'), 'batch'), may hold values from -0.1875 to 0.1875
- weight: bfloat16 [4096, 8192], P(('hidden', 'solver'), 'batch'), may hold values from -0.09375 to 0.09375
- left_old: float32 [4, 8, 1024, 1024], P('hidden', 'batch'), may hold values from -0.001953125 to 2.0019531, as said below
- right_old: float32 [4, 8, 1024, 1024], P('hidden', 'batch'), may hold values from -0.001953125 to 2.0019531, as said below
Outputs:
- first_out: bfloat16 [8192, 1024], P(('hidden', 'solver'), 'batch')
- new_left: float32 [4, 8, 1024, 1024], P('hidden', 'batch', 'solver')
- new_right: float32 [4, 8, 1024, 1024], P('hidden', 'batch', 'solver')
- direction: float32 [4096, 8192], P(('hidden', 'solver'), 'batch')
- second_out: bfloat16 [8192, 1024], P(('hidden', 'solver'), 'batch')
Inputs may be any that keep to these rules, and one draw needn't show every extreme that they name: `activations`: in the hidden draw each feature carries its own scale. `left_old`: every block is symmetric, its diagonal is positive and larger than the sum of the magnitudes of the rest of its row. `right_old`: every block is symmetric, its diagonal is positive and larger than the sum of the magnitudes of the rest of its row.
All inputs are finite; a program needn't handle non-finite values. Where the computation divides by a largest or mean magnitude, that divisor is 1e-20 or more.
Results may differ from a plain program's by a relative error of at most 0.017.
Values may be sent and summed in bfloat16 or wider, within the bound.
A program may use at most 128 MiB of HBM per device.

v0:
```python
import jax
import jax.numpy as jnp
from jax import lax
from jax.sharding import PartitionSpec as P

BLOCK = 1024


STAT_DECAY = 0.8
LEARN_RATE = 0.005
EPSILON = 1e-06


def product(left_mat, right_mat):
    return jnp.einsum(
        "bij,bjk->bik",
        left_mat,
        right_mat,
        precision=lax.Precision.HIGHEST,
        preferred_element_type=jnp.float32,
    )


def prepare(factor):
    identity = jnp.eye(BLOCK, dtype=jnp.float32)
    scaled = 2.5 / (jnp.max(jnp.sum(jnp.abs(factor), axis=2), axis=1) + EPSILON)
    moment = scaled[:, None, None] * factor
    newton_step = (5.0 * identity - moment) * 0.25
    return (scaled, moment, newton_step)


def transposed_product(weight_cols, acts):
    return lax.dot_general(
        weight_cols, acts, (((0,), (1,)), ((), ())), preferred_element_type=jnp.float32
    )


def body(activations, cotangent, weight, left_old, right_old):
    rows_here = weight.shape[0]
    nblocks = weight.shape[1] // BLOCK
    weight_rows = lax.all_gather(weight, "batch", axis=1, tiled=True)
    columns = weight_rows
    first_sum = lax.psum_scatter(
        transposed_product(columns, activations).astype(jnp.bfloat16),
        ("hidden", "solver"),
        scatter_dimension=0,
        tiled=True,
    )
    cotangent_all = lax.all_gather(cotangent, ("hidden", "solver"), axis=0, tiled=True)
    grad_local = lax.psum_scatter(
        jnp.dot(cotangent_all, activations, preferred_element_type=jnp.float32).astype(
            jnp.bfloat16
        ),
        "batch",
        scatter_dimension=0,
        tiled=True,
    )
    grad_blocks = grad_local.reshape(nblocks, BLOCK, rows_here)
    grad_full = lax.all_gather(grad_blocks, "solver", axis=2, tiled=True)
    gram_left = jnp.einsum("bnm,bnk->bmk", grad_full, grad_full, preferred_element_type=jnp.float32)
    gram_right = jnp.einsum(
        "bnm,bkm->bnk", grad_full, grad_full, preferred_element_type=jnp.float32
    )
    left_all = STAT_DECAY * left_old[0] + (1.0 - STAT_DECAY) / BLOCK * gram_left
    right_all = STAT_DECAY * right_old[0] + (1.0 - STAT_DECAY) / BLOCK * gram_right
    first_row = lax.axis_index("solver") * rows_here
    new_left = lax.dynamic_slice_in_dim(left_all, first_row, rows_here, 1)[None]
    new_right = lax.dynamic_slice_in_dim(right_all, first_row, rows_here, 1)[None]
    scale_left, moment_left, step_left = prepare(left_all)
    own_rows = lax.dynamic_slice_in_dim(step_left, first_row, rows_here, 1)
    power_rows = product(
        product(product(product(own_rows, step_left), step_left), step_left), moment_left
    )
    row_index = lax.broadcasted_iota(jnp.int32, (rows_here, BLOCK), 0) + first_row
    col_index = lax.broadcasted_iota(jnp.int32, (rows_here, BLOCK), 1)
    eye_rows = (row_index == col_index).astype(jnp.float32)
    next_rows = (5.0 * eye_rows - power_rows) * 0.25
    root_rows = (scale_left**0.25)[:, None, None] * product(next_rows, step_left)
    grad_float = grad_full.astype(jnp.float32)
    mixed_rows = jnp.einsum(
        "brm,bnm->brn",
        root_rows,
        grad_float,
        precision=lax.Precision.HIGHEST,
        preferred_element_type=jnp.float32,
    )
    scale_right, moment_right, step_right = prepare(right_all)
    turned = product(mixed_rows, step_right)
    power_right = product(
        product(product(product(product(turned, step_right), step_right), step_right), step_right),
        moment_right,
    )
    update = (scale_right**0.25)[:, None, None] * ((5.0 * turned - power_right) * 0.25)
    squares = lax.psum(jnp.sum(update * update, axis=(1, 2)), "solver")
    spread = jnp.sqrt(squares / (BLOCK * BLOCK) + EPSILON)
    scaled_update = update / spread[:, None, None]
    direction = jnp.transpose(scaled_update, (1, 0, 2)).reshape(rows_here, nblocks * BLOCK)
    new_weight = (weight.astype(jnp.float32) - LEARN_RATE * direction).astype(jnp.bfloat16)
    new_rows = lax.all_gather(new_weight, "batch", axis=1, tiled=True)
    columns = new_rows
    second_sum = lax.psum_scatter(
        transposed_product(columns, activations).astype(jnp.bfloat16),
        ("hidden", "solver"),
        scatter_dimension=0,
        tiled=True,
    )
    return (first_sum, new_left, new_right, direction, second_sum)


def solution(mesh):
    in_specs = (
        P("batch", ("hidden", "solver")),
        P(("hidden", "solver"), "batch"),
        P(("hidden", "solver"), "batch"),
        P("hidden", "batch", None, None),
        P("hidden", "batch", None, None),
    )
    out_specs = (
        P(("hidden", "solver"), "batch"),
        P("hidden", "batch", "solver", None),
        P("hidden", "batch", "solver", None),
        P(("hidden", "solver"), "batch"),
        P(("hidden", "solver"), "batch"),
    )
    return jax.shard_map(body, mesh=mesh, in_specs=in_specs, out_specs=out_specs, check_vma=False)
```

profile of v0, /device:TPU:4, one launch (start us, length us, event | category | flops | bytes accessed | tf_op | source)
XLA Modules:
  0.0 719.7 jit_solution(6583412201741329409)
XLA Ops:
  8.0 75.3 %all-gather.7.cloned.1.call-done = bf16[8192,256]{1,0:T(8,128)(2,1)} async-done(((bf16[1024,256]{1,0:T(8,128)(2,1)}), bf16[8192,256]{1,0:T(8,128)(2,1)}) %all-gather.7.cloned.1.call-update) | async-done | bytes 4194320 | tf_op jit(solution)/shard_map/all_gather | solution.py:49
  83.2 7.8 %convolution_convert_fusion = bf16[8192,512]{1,0:T(8,128)(2,1)} fusion(bf16[8192,256]{1,0:T(8,128)(2,1)} %all-gather.7.cloned.1.call-done, bf16[256,512]{1,0:T(8,128)(2,1)S(1)} %copy-done), kind=kOutput, calls=%fused_computation | convolution fusion | flops 2151677952 | bytes 12845056 | tf_op jit(solution)/shard_map/dot_general | solution.py:51
  91.1 71.0 %reduce-scatter.6.cloned.1.call-done = bf16[2048,512]{1,0:T(8,128)(2,1)} async-done(((bf16[8192,512]{1,0:T(8,128)(2,1)}), bf16[2048,512]{1,0:T(8,128)(2,1)}) %reduce-scatter.6.cloned.1.call-update) | async-done | bytes 2097168 | tf_op jit(solution)/shard_map/reduce_scatter | solution.py:50
  172.1 9.1 %copy.31 = f32[1,2,1024,1024]{2,3,1,0:T(8,128)} copy(f32[1,2,1024,1024]{3,2,1,0:T(8,128)} %param.8) | data formatting | bytes 16777216 | tf_op args[3]
  181.2 8.7 %copy.35 = f32[1,2,1024,1024]{2,3,1,0:T(8,128)} copy(f32[1,2,1024,1024]{3,2,1,0:T(8,128)} %param.9) | data formatting | bytes 16777216 | tf_op args[4]
  190.2 31.6 %all-gather.9.cloned.1.call-done = bf16[2,1024,1024]{1,2,0:T(8,128)(2,1)} async-done(((bf16[2,1024,512]{1,2,0:T(8,128)(2,1)}), bf16[2,1024,1024]{1,2,0:T(8,128)(2,1)}) %all-gather.9.cloned.1.call-update) | async-done | bytes 4194320 | tf_op jit(solution)/shard_map/all_gather | solution.py:59
  221.7 15.7 %abs_reduce_fusion.1 = (f32[2,1024]{1,0:T(2,128)S(1)}, f32[2,1024,1024]{1,2,0:T(8,128)}) fusion(bf16[2,1024,1024]{1,2,0:T(8,128)(2,1)} %all-gather.9.cloned.1.call-done, f32[1,2,1024,1024]{2,3,1,0:T(8,128)} %copy.31), kind=kOutput, calls=%fused_computation.8 | convolution fusion | flops 4305451008 | bytes 20979712 | tf_op jit(solution)/shard_map/bnm,bnk->bmk/dot_general | solution.py:60
  237.4 10.1 %abs_reduce_fusion = (f32[2,1024]{1,0:T(2,128)S(1)}, f32[2,1024,1024]{1,2,0:T(8,128)}) fusion(bf16[2,1024,1024]{1,2,0:T(8,128)(2,1)S(1)} %copy-done.4, f32[1,2,1024,1024]{2,3,1,0:T(8,128)} %copy.35), kind=kOutput, calls=%fused_computation.6 | convolution fusion | flops 4305451008 | bytes 20979712 | tf_op jit(solution)/shard_map/bnm,bkm->bnk/dot_general | solution.py:61
  247.8 11.6 %subtract_multiply_fusion = (f32[2,1024,1024]{1,2,0:T(8,128)S(1)}, f32[2,1024,1024]{1,2,0:T(8,128)}) fusion(f32[2,1024,1024]{1,2,0:T(8,128)} %get-tuple-element.22, f32[2]{0:T(128)S(1)} %get-tuple-element.16, f32[1024,1024]{0,1:T(8,128)} %fusion.13, f32[2,1024,1024]{1,2,0:T(8,128)} %get-tuple-element.24, f32[2]{0:T(128)S(1)} %get-tuple-element.28), kind=kLoop, calls=%fused_computation.5 | loop fusion | flops 12582912 | bytes 37748752 | tf_op jit(solution)/shard_map/mul | solution.py:28
  259.4 31.3 %fusion.10 = f32[2,512,1024]{2,1,0:T(8,128)S(1)} fusion(f32[2,1024,1024]{1,2,0:T(8,128)} %get-tuple-element.20, s32[]{:T(128)S(6)} %select_n.2), kind=kOutput, calls=%fused_computation.23 | convolution fusion | flops 12884901888 | bytes 16777220 | tf_op jit(solution)/shard_map/bij,bjk->bik/dot_general | solution.py:15
  290.7 14.3 %fusion.22 = f32[2,512,1024]{2,1,0:T(8,128)S(1)} fusion(f32[2,512,1024]{2,1,0:T(8,128)S(1)} %fusion.10, f32[2,1024,1024]{1,2,0:T(8,128)S(1)} %copy-done.1), kind=kOutput, calls=%fused_computation.43 | convolution fusion | flops 12884901888 | bytes 16777216 | tf_op jit(solution)/shard_map/bij,bjk->bik/dot_general | solution.py:15
  304.9 14.3 %fusion.23 = f32[2,512,1024]{2,1,0:T(8,128)S(1)} fusion(f32[2,512,1024]{2,1,0:T(8,128)S(1)} %fusion.22, f32[2,1024,1024]{1,2,0:T(8,128)S(1)} %copy-done.1), kind=kOutput, calls=%fused_computation.44 | convolution fusion | flops 12884901888 | bytes 16777216 | tf_op jit(solution)/shard_map/bij,bjk->bik/dot_general | solution.py:15
  319.3 16.3 %fusion.2 = f32[2,512,1024]{2,1,0:T(8,128)S(1)} fusion(f32[2,512,1024]{2,1,0:T(8,128)S(1)} %fusion.23, f32[2,1024,1024]{1,2,0:T(8,128)} %get-tuple-element.24, f32[2]{0:T(128)S(1)} %get-tuple-element.28), kind=kOutput, calls=%fused_computation.11 | convolution fusion | flops 12886999040 | bytes 16777224 | tf_op jit(solution)/shard_map/bij,bjk->bik/dot_general | solution.py:15
  335.6 15.6 %fusion.7 = f32[2,512,1024]{2,1,0:T(8,128)} fusion(f32[2,1024,1024]{1,2,0:T(8,128)S(1)} %copy-done.1, f32[2,512,1024]{2,1,0:T(8,128)S(1)} %fusion.2, f32[512,1024]{1,0:T(8,128)S(1)} %fusion.17), kind=kOutput, calls=%fused_computation.20 | convolution fusion | flops 12886999040 | bytes 18874368 | tf_op jit(solution)/shard_map/bij,bjk->bik/dot_general | solution.py:15
  351.2 9.4 %fusion.5 = f32[2,512,1024]{2,1,0:T(8,128)S(1)} fusion(bf16[2,1024,1024]{1,2,0:T(8,128)(2,1)} %all-gather.9.cloned.1.call-done, f32[2,512,1024]{2,1,0:T(8,128)} %fusion.7, f32[2]{0:T(128)S(1)} %get-tuple-element.27), kind=kOutput, calls=%fused_computation.18 | convolution fusion | flops 12885950464 | bytes 12582920 | tf_op jit(solution)/shard_map/brm,bnm->brn/dot_general | solution.py:80
  360.6 14.3 %fusion.24 = f32[2,512,1024]{2,1,0:T(8,128)S(1)} fusion(f32[2,512,1024]{2,1,0:T(8,128)S(1)} %fusion.5, f32[2,1024,1024]{1,2,0:T(8,128)S(1)} %get-tuple-element.19), kind=kOutput, calls=%fused_computation.45 | convolution fusion | flops 12884901888 | bytes 16777216 | tf_op jit(solution)/shard_map/bij,bjk->bik/dot_general | solution.py:15
  374.9 14.6 %fusion.25 = f32[2,512,1024]{2,1,0:T(8,128)S(1)} fusion(f32[2,512,1024]{2,1,0:T(8,128)S(1)} %fusion.24, f32[2,1024,1024]{1,2,0:T(8,128)S(1)} %get-tuple-element.19), kind=kOutput, calls=%fused_computation.46 | convolution fusion | flops 12884901888 | bytes 16777216 | tf_op jit(solution)/shard_map/bij,bjk->bik/dot_general | solution.py:15
  389.5 14.3 %fusion.26 = f32[2,512,1024]{2,1,0:T(8,128)S(1)} fusion(f32[2,512,1024]{2,1,0:T(8,128)S(1)} %fusion.25, f32[2,1024,1024]{1,2,0:T(8,128)S(1)} %get-tuple-element.19), kind=kOutput, calls=%fused_computation.47 | convolution fusion | flops 12884901888 | bytes 16777216 | tf_op jit(solution)/shard_map/bij,bjk->bik/dot_general | solution.py:15
  403.8 14.4 %fusion.27 = f32[2,512,1024]{2,1,0:T(8,128)S(1)} fusion(f32[2,512,1024]{2,1,0:T(8,128)S(1)} %fusion.26, f32[2,1024,1024]{1,2,0:T(8,128)S(1)} %get-tuple-element.19), kind=kOutput, calls=%fused_computation.48 | convolution fusion | flops 12884901888 | bytes 16777216 | tf_op jit(solution)/shard_map/bij,bjk->bik/dot_general | solution.py:15
  418.2 14.7 %fusion.28 = f32[2,512,1024]{2,1,0:T(8,128)S(1)} fusion(f32[2,512,1024]{2,1,0:T(8,128)S(1)} %fusion.27, f32[2,1024,1024]{1,2,0:T(8,128)S(1)} %get-tuple-element.19), kind=kOutput, calls=%fused_computation.49 | convolution fusion | flops 12884901888 | bytes 16777216 | tf_op jit(solution)/shard_map/bij,bjk->bik/dot_general | solution.py:15
  433.0 16.0 %multiply_reduce_fusion = (f32[2]{0:T(128)S(1)}, f32[2,512,1024]{2,1,0:T(8,128)}) fusion(f32[2]{0:T(128)S(1)} %get-tuple-element.15, f32[2,512,1024]{2,1,0:T(8,128)S(1)} %fusion.28, f32[2,1024,1024]{1,2,0:T(8,128)S(1)} %bitcast.41, f32[2]{0:T(128)S(1)} %get-tuple-element.16, f32[2,512,1024]{2,1,0:T(8,128)S(1)} %fusion.24), kind=kOutput, calls=%fused_computation.15 | convolution fusion | flops 12892241920 | bytes 20971544 | tf_op jit(solution)/shard_map/bij,bjk->bik/dot_general | solution.py:15
  449.0 4.9 psum.7
  453.9 5.1 divide_bitcast_fusion
  459.0 5.5 copy.52
  468.8 7.9 %convolution_convert_fusion.2 = bf16[8192,256]{1,0:T(8,128)(2,1)} fusion(bf16[512,8192]{1,0:T(8,128)(2,1)} %all-gather.5.cloned.1.call-done, bf16[256,512]{1,0:T(8,128)(2,1)S(1)} %copy-done), kind=kOutput, calls=%fused_computation.2 | convolution fusion | flops 2149580800 | bytes 12845056 | tf_op jit(solution)/shard_map/dot_general | solution.py:33
  477.0 51.1 %all-gather.11.cloned.1.call-done = bf16[512,8192]{0,1:T(8,128)(2,1)} async-done(((bf16[512,2048]{0,1:T(8,128)(2,1)}), bf16[512,8192]{0,1:T(8,128)(2,1)}) %all-gather.11.cloned.1.call-update) | async-done | bytes 8388624 | tf_op jit(solution)/shard_map/all_gather | solution.py:99
  528.1 7.7 %convolution_convert_fusion.1 = bf16[8192,256]{1,0:T(8,128)(2,1)} fusion(bf16[512,8192]{0,1:T(8,128)(2,1)} %all-gather.11.cloned.1.call-done, bf16[256,512]{1,0:T(8,128)(2,1)S(1)} %copy-done), kind=kOutput, calls=%fused_computation.1 | convolution fusion | flops 2149580800 | bytes 12845056 | tf_op jit(solution)/shard_map/dot_general | solution.py:33
  535.8 5.4 copy.54
  545.8 5.4 copy.34
  555.8 5.5 copy.38
  561.3 59.2 %reduce-scatter.4.cloned.1.call-done = bf16[1024,256]{1,0:T(8,128)(2,1)} async-done(((bf16[8192,256]{1,0:T(8,128)(2,1)}), bf16[1024,256]{1,0:T(8,128)(2,1)}) %reduce-scatter.4.cloned.1.call-update) | async-done | bytes 524304 | tf_op jit(solution)/shard_map/reduce_scatter | solution.py:43
  620.5 92.1 %reduce-scatter.8.cloned.1.call-done = bf16[1024,256]{1,0:T(8,128)(2,1)} async-done(((bf16[8192,256]{1,0:T(8,128)(2,1)}), bf16[1024,256]{1,0:T(8,128)(2,1)}) %reduce-scatter.8.cloned.1.call-update) | async-done | bytes 524304 | tf_op jit(solution)/shard_map/reduce_scatter | solution.py:101
  (42 shorter events, 25.3 us)
Async XLA Ops:
  7.2 76.1 %copy-start = (bf16[256,512]{1,0:T(8,128)(2,1)S(1)}, bf16[256,512]{1,0:T(8,128)(2,1)}, u32[]{:S(2)}) copy-start(bf16[256,512]{1,0:T(8,128)(2,1)} %param.5) | copy-start | bytes 786436
  7.2 76.0 %all-gather.7.cloned.1.call-start = ((), (), s32[]{:S(2)}) async-start(), calls=%async_computation.5 | async-start | bytes 4718592 | tf_op jit(solution)/shard_map/all_gather | solution.py:49
  7.9 154.1 %reduce-scatter.6.cloned.1.call-start = ((), (), s32[]{:S(2)}) async-start(), calls=%async_computation.6 | async-start | bytes 10485760 | tf_op jit(solution)/shard_map/reduce_scatter | solution.py:50
  91.0 130.7 %all-gather.9.cloned.1.call-start = ((), (), s32[]{:S(2)}) async-start(), calls=%async_computation.7 | async-start | bytes 6291456 | tf_op jit(solution)/shard_map/all_gather | solution.py:59
  166.0 3.7 copy-start.2
  166.0 302.8 %all-gather.5.cloned.1.call-start = ((), (), s32[]{:S(2)}) async-start(), calls=%async_computation.3 | async-start | bytes 10485760 | tf_op jit(solution)/shard_map/all_gather | solution.py:41
  166.6 361.5 %all-gather.11.cloned.1.call-start = ((), (), s32[]{:S(2)}) async-start(), calls=%async_computation.8 | async-start | bytes 10485760 | tf_op jit(solution)/shard_map/all_gather | solution.py:99
  221.7 15.7 %copy-start.4 = (bf16[2,1024,1024]{1,2,0:T(8,128)(2,1)S(1)}, bf16[2,1024,1024]{1,2,0:T(8,128)(2,1)}, u32[]{:S(2)}) copy-start(bf16[2,1024,1024]{1,2,0:T(8,128)(2,1)} %all-gather.9.cloned.1.call-done) | copy-start | bytes 12582916
  259.3 31.3 %copy-start.1 = (f32[2,1024,1024]{1,2,0:T(8,128)S(1)}, f32[2,1024,1024]{1,2,0:T(8,128)}, u32[]{:S(2)}) copy-start(f32[2,1024,1024]{1,2,0:T(8,128)} %get-tuple-element.20) | copy-start | bytes 25165828
  403.8 29.1 %slice-start = ((s8[8388608]{0:T(1024)(128)(4,1)}), s8[4194304]{0:T(1024)(128)(4,1)S(1)}, s32[]{:S(2)}) async-start(s8[8388608]{0:T(1024)(128)(4,1)} %bitcast.40), calls=%async_computation.10 | async-start | bytes 8388608
  418.2 14.7 %slice-start.1 = ((s8[8388608]{0:T(1024)(128)(4,1)}), s8[4194304]{0:T(1024)(128)(4,1)S(1)}, s32[]{:S(2)}) async-start(s8[8388608]{0:T(1024)(128)(4,1)} %bitcast.40), calls=%async_computation.11 | async-start | bytes 8388608
  459.0 5.5 copy-start.3
  468.8 151.7 %reduce-scatter.4.cloned.1.call-start = ((), (), s32[]{:S(2)}) async-start(), calls=%async_computation.4 | async-start | bytes 4718592 | tf_op jit(solution)/shard_map/reduce_scatter | solution.py:43
  476.7 235.9 %reduce-scatter.8.cloned.1.call-start = ((), (), s32[]{:S(2)}) async-start(), calls=%async_computation.9 | async-start | bytes 4718592 | tf_op jit(solution)/shard_map/reduce_scatter | solution.py:101
Sparse Core Ops, SparseCore 0:
  10.1 73.0 all-gather.6
  91.1 70.8 reduce-scatter.5
  166.1 55.5 all-gather.8
  223.1 59.3 all-gather.4
  468.9 59.1 all-gather.10
  532.2 88.2 reduce-scatter.3
  624.7 87.8 reduce-scatter.7
where the time goes:
time: 725 us; the launch traced here: 720 us
  waiting for transfers between devices  382 us (53%)
  matrix products  239 us (33%)
  local copies, waits for them, and re-layouts  55.2 us (8%)
  other arithmetic  23.9 us (3%)
  between operations  14.5 us (2%)
    dot_general x11, matrix products, product(): jnp.einsum('bij,bjk->bik', left_mat, right_mat, precision=lax.Precision.H...  180 us
    reduce_scatter x2, waiting for transfers between devices, body(): lax.psum_scatter(transposed_product(columns, activations).astype(jnp.bflo...  151 us
    all_gather x1, waiting for transfers between devices, body(): lax.all_gather(cotangent, ('hidden', 'solver'), axis=0, tiled=True)  75.3 us
    reduce_scatter x1, waiting for transfers between devices, body(): lax.psum_scatter(jnp.dot(cotangent_all, activations, preferred_element_ty...  71 us
    all_gather x1, waiting for transfers between devices, body(): new_rows = lax.all_gather(new_weight, 'batch', axis=1, tiled=True)  51.1 us
    all_gather x1, waiting for transfers between devices, body(): grad_full = lax.all_gather(grad_blocks, 'solver', axis=2, tiled=True)  31.6 us
    unnamed x18, local copies, waits for them, and re-layouts  25.7 us
    dot_general x1, matrix products, body(): jnp.einsum('bnm,bnk->bmk', grad_full, grad_full, preferred_element_type=j...  15.7 us
  transfers between devices with their start and end apart: 7, of which 6 were waited for; matrix products, arithmetic and copies ran while one was open for 43% of the time, Pallas kernels for 0%

commit v1 on v0

v1 whole, which is shorter than its diff:
```python
import jax
import jax.numpy as jnp
from jax import lax
from jax.sharding import PartitionSpec as P

BLOCK = 1024


STAT_DECAY = 0.8
LEARN_RATE = 0.005
EPSILON = 1e-06

ALL = ("batch", "hidden", "solver")
FEATURES = ("hidden", "solver")


def product(left_mat, right_mat):
    return jnp.einsum("bij,bjk->bik", left_mat, right_mat, preferred_element_type=jnp.float32)


def prepare(factor):
    identity = jnp.eye(BLOCK, dtype=jnp.float32)
    scaled = 2.5 / (jnp.max(jnp.sum(jnp.abs(factor), axis=2), axis=1) + EPSILON)
    moment = scaled[:, None, None] * factor
    newton_step = (5.0 * identity - moment) * 0.25
    return (scaled, moment.astype(jnp.bfloat16), newton_step.astype(jnp.bfloat16))


def apply_root(start, moment, step):
    power = start
    for _ in range(4):
        power = product(power.astype(jnp.bfloat16), step)
    power = product(power.astype(jnp.bfloat16), moment)
    return (5.0 * start.astype(jnp.float32) - power) * 0.25


def body(activations, cotangent, weight, left_old, right_old, *, n_batch, n_feat):
    rows_here = weight.shape[0]
    nblocks = weight.shape[1] // BLOCK
    per_batch = n_feat // n_batch
    out_rows = weight.shape[1] // per_batch
    tokens = activations.shape[0]
    to_owner = [
        (b * n_feat + c * n_batch + t, t * n_feat + b * per_batch + c)
        for b in range(n_batch)
        for c in range(per_batch)
        for t in range(n_batch)
    ]
    from_owner = [(target, source) for source, target in to_owner]

    def partial_forward(weight_here):
        split = weight_here.reshape(rows_here, per_batch, out_rows)
        out = jnp.einsum("fco,btf->cbot", split, acts_all, preferred_element_type=jnp.float32)
        return out.astype(jnp.bfloat16).reshape(n_feat * out_rows, tokens)

    def reduce_forward(partial):
        return lax.psum_scatter(partial, FEATURES, scatter_dimension=0, tiled=True)

    acts_all = lax.all_gather(activations, "batch", axis=0, tiled=False)
    acts_block = lax.all_gather(acts_all, "solver", axis=2, tiled=True)
    cot_moved = lax.ppermute(cotangent, ALL, from_owner)
    cot_all = lax.all_gather(cot_moved, FEATURES, axis=0, tiled=False)
    cot_all = cot_all.reshape(per_batch, n_batch, out_rows, tokens)
    first_partial = partial_forward(weight)
    first_partial, cot_all = lax.optimization_barrier((first_partial, cot_all))
    first_sum = reduce_forward(first_partial)
    grad_full = jnp.einsum("cbot,btf->cof", cot_all, acts_block, preferred_element_type=jnp.float32)
    grad_full = grad_full.astype(jnp.bfloat16).reshape(nblocks, BLOCK, BLOCK)
    gram_left = jnp.einsum("bnm,bnk->bmk", grad_full, grad_full, preferred_element_type=jnp.float32)
    gram_right = jnp.einsum(
        "bnm,bkm->bnk", grad_full, grad_full, preferred_element_type=jnp.float32
    )
    left_all = STAT_DECAY * left_old[0] + (1.0 - STAT_DECAY) / BLOCK * gram_left
    right_all = STAT_DECAY * right_old[0] + (1.0 - STAT_DECAY) / BLOCK * gram_right
    first_row = lax.axis_index("solver") * rows_here
    new_left = lax.dynamic_slice_in_dim(left_all, first_row, rows_here, 1)[None]
    new_right = lax.dynamic_slice_in_dim(right_all, first_row, rows_here, 1)[None]
    scale_left, moment_left, step_left = prepare(left_all)
    own_rows = lax.dynamic_slice_in_dim(step_left, first_row, rows_here, 1)
    root_rows = apply_root(own_rows, moment_left, step_left)
    mixed_rows = jnp.einsum(
        "brm,bnm->brn",
        root_rows.astype(jnp.bfloat16),
        grad_full,
        preferred_element_type=jnp.float32,
    )
    scale_right, moment_right, step_right = prepare(right_all)
    turned = product(mixed_rows.astype(jnp.bfloat16), step_right)
    scale_both = (scale_left**0.25) * (scale_right**0.25)
    update = scale_both[:, None, None] * apply_root(turned, moment_right, step_right)
    update, first_sum = lax.optimization_barrier((update, first_sum))
    first_out = lax.ppermute(first_sum, ALL, to_owner)
    squares = lax.psum(jnp.sum(update * update, axis=(1, 2)), "solver")
    spread = jnp.sqrt(squares / (BLOCK * BLOCK) + EPSILON)
    scaled_update = update / spread[:, None, None]
    direction = jnp.transpose(scaled_update, (1, 0, 2)).reshape(rows_here, nblocks * BLOCK)
    new_weight = (weight.astype(jnp.float32) - LEARN_RATE * direction).astype(jnp.bfloat16)
    second_sum = reduce_forward(partial_forward(new_weight))
    second_out = lax.ppermute(second_sum, ALL, to_owner)
    return (first_out, new_left, new_right, direction, second_out)


def solution(mesh):
    in_specs = (
        P("batch", ("hidden", "solver")),
        P(("hidden", "solver"), "batch"),
        P(("hidden", "solver"), "batch"),
        P("hidden", "batch", None, None),
        P("hidden", "batch", None, None),
    )
    out_specs = (
        P(("hidden", "solver"), "batch"),
        P("hidden", "batch", "solver", None),
        P("hidden", "batch", "solver", None),
        P(("hidden", "solver"), "batch"),
        P(("hidden", "solver"), "batch"),
    )
    n_batch = mesh.shape["batch"]
    n_feat = mesh.shape["hidden"] * mesh.shape["solver"]

    def step(activations, cotangent, weight, left_old, right_old):
        return body(
            activations, cotangent, weight, left_old, right_old, n_batch=n_batch, n_feat=n_feat
        )

    return jax.shard_map(step, mesh=mesh, in_specs=in_specs, out_specs=out_specs, check_vma=False)
```

time: 725 us -> 450 us (0.62)
  waiting for transfers between devices: 382 us -> 227 us
  matrix products: 239 us -> 106 us
  starting transfers between devices: 1.02 us -> 8.62 us
    dot_general x15 -> x10, matrix products: 213 us -> 84.7 us  [the longest x7 67 us: product(): jnp.einsum('bij,bjk->bik', left_mat, right_mat, preferred_element_type=jn...]
    reduce_scatter x3 -> x2, waiting for transfers between devices: 222 us -> 107 us  [reduce_forward(): return lax.psum_scatter(partial, FEATURES, scatter_dimension=0, tiled=True)]
    all_gather x4 -> x3, waiting for transfers between devices: 158 us -> 97.1 us  [the longest x1 62.3 us: body(): cot_all = lax.all_gather(cot_moved, FEATURES, axis=0, tiled=False)]
    ppermute x0 -> x3, waiting for transfers between devices: none -> 21.4 us  [the longest x1 12.1 us: body(): cot_moved = lax.ppermute(cotangent, ALL, from_owner)]
    convert_element_type x0 -> x1, other arithmetic: none -> 12.6 us  [prepare(): newton_step.astype(jnp.bfloat16)]
    mul x2 -> x1, other arithmetic: 14.1 us -> 2.52 us  [prepare(): newton_step = (5.0 * identity - moment) * 0.25]
    ppermute x0 -> x3, starting transfers between devices: none -> 8.26 us  [the longest x1 4.44 us: body(): cot_moved = lax.ppermute(cotangent, ALL, from_owner)]
    unnamed x18 -> x15, local copies, waits for them, and re-layouts: 25.7 us -> 26.6 us
  transfers between devices with their start and end apart: 7 -> 8, of which waited for: 6 -> 6; matrix products, arithmetic and copies ran while one was open for 43% -> 36% of each run, Pallas kernels for 0% -> 0%
where the time goes in v1:
time: 450 us; the launch traced here: 446 us
  waiting for transfers between devices  227 us (50%)
  matrix products  106 us (24%)
  local copies, waits for them, and re-layouts  59.3 us (13%)
  other arithmetic  26.6 us (6%)
  between operations  14.1 us (3%)
  starting transfers between devices  8.62 us (2%)
  blocking collectives  4.92 us (1%)
    reduce_scatter x2, waiting for transfers between devices, reduce_forward(): return lax.psum_scatter(partial, FEATURES, scatter_dimension=0, tiled=True)  107 us
    dot_general x7, matrix products, product(): jnp.einsum('bij,bjk->bik', left_mat, right_mat, preferred_element_type=jn...  67 us
    all_gather x1, waiting for transfers between devices, body(): cot_all = lax.all_gather(cot_moved, FEATURES, axis=0, tiled=False)  62.3 us
    all_gather x1, waiting for transfers between devices, body(): acts_block = lax.all_gather(acts_all, 'solver', axis=2, tiled=True)  32.8 us
    unnamed x15, local copies, waits for them, and re-layouts  26.6 us
    dynamic_slice x2, local copies, waits for them, and re-layouts, body(): lax.dynamic_slice_in_dim(right_all, first_row, rows_here, 1)[None]  13.1 us
    convert_element_type x1, other arithmetic, prepare(): newton_step.astype(jnp.bfloat16)  12.6 us
    ppermute x1, waiting for transfers between devices, body(): cot_moved = lax.ppermute(cotangent, ALL, from_owner)  12.1 us
  transfers between devices with their start and end apart: 8, of which 6 were waited for; matrix products, arithmetic and copies ran while one was open for 36% of the time, Pallas kernels for 0%

profile of v1, /device:TPU:4, one launch (start us, length us, event | category | flops | bytes accessed | tf_op | source)
XLA Modules:
  0.0 445.9 jit_solution(5981928207677267999)
XLA Ops:
  7.9 4.4 collective-permute-start
  12.4 12.1 %collective-permute-done = bf16[1024,256]{1,0:T(8,128)(2,1)S(1)} collective-permute-done((bf16[1024,256]{1,0:T(8,128)(2,1)}, bf16[1024,256]{1,0:T(8,128)(2,1)S(1)}, u32[]{:S(2)}, u32[]{:S(2)}) %collective-permute-start) | collective-permute-done | bytes 524320 | tf_op jit(solution)/shard_map/ppermute | solution.py:61
  27.5 8.7 %copy.35 = f32[1,2,1024,1024]{2,3,1,0:T(8,128)} copy(f32[1,2,1024,1024]{3,2,1,0:T(8,128)} %param.8) | data formatting | bytes 16777216 | tf_op args[3]
  36.2 8.7 %copy.47 = f32[1,2,1024,1024]{2,3,1,0:T(8,128)} copy(f32[1,2,1024,1024]{3,2,1,0:T(8,128)} %param.9) | data formatting | bytes 16777216 | tf_op args[4]
  44.9 2.5 fusion.4
  47.8 4.4 convert_bitcast_fusion
  52.2 6.3 %copy.37 = bf16[2,4,1024,256]{3,2,1,0:T(8,128)(2,1)} copy(bf16[2,4,1024,256]{2,3,0,1:T(8,128)(2,1)} %convert_bitcast_fusion) | data formatting | bytes 8388608 | tf_op jit(solution)/shard_map/convert_element_type | solution.py:54
  58.5 62.3 %all-gather.10.cloned.1.call-done = bf16[8192,256]{1,0:T(8,128)(2,1)} async-done(((bf16[1024,256]{1,0:T(8,128)(2,1)}), bf16[8192,256]{1,0:T(8,128)(2,1)}) %all-gather.10.cloned.1.call-update) | async-done | bytes 4194320 | tf_op jit(solution)/shard_map/all_gather | solution.py:62
  121.0 32.8 %all-gather.6.cloned.1.call-done = bf16[4,256,1024]{2,1,0:T(8,128)(2,1)} async-done(((bf16[4,256,512]{2,1,0:T(8,128)(2,1)}), bf16[4,256,1024]{2,1,0:T(8,128)(2,1)}) %all-gather.6.cloned.1.call-update) | async-done | bytes 2097168 | tf_op jit(solution)/shard_map/all_gather | solution.py:60
  153.8 7.4 %bitcast_convert_fusion = bf16[2,1024,1024]{2,1,0:T(8,128)(2,1)S(1)} fusion(bf16[2,4,1024,256]{3,2,1,0:T(8,128)(2,1)} %bitcast.71, bf16[4,256,1024]{2,1,0:T(8,128)(2,1)} %all-gather.6.cloned.1.call-done), kind=kOutput, calls=%fused_computation.1 | convolution fusion | flops 4297064448 | bytes 10485760 | tf_op jit(solution)/shard_map/cbot,btf->cof/dot_general | solution.py:67
  161.2 11.6 %abs_reduce_fusion.1 = (f32[2,1024]{1,0:T(2,128)S(1)}, f32[2,1024,1024]{1,2,0:T(8,128)}) fusion(bf16[2,1024,1024]{2,1,0:T(8,128)(2,1)S(1)} %bitcast_convert_fusion, f32[1,2,1024,1024]{2,3,1,0:T(8,128)} %copy.35), kind=kOutput, calls=%fused_computation.6 | convolution fusion | flops 4305451008 | bytes 20979712 | tf_op jit(solution)/shard_map/bnm,bnk->bmk/dot_general | solution.py:69
  172.8 9.5 %abs_reduce_fusion = (f32[2,1024]{1,0:T(2,128)S(1)}, f32[2,1024,1024]{1,2,0:T(8,128)}) fusion(bf16[2,1024,1024]{2,1,0:T(8,128)(2,1)S(1)} %bitcast_convert_fusion, f32[1,2,1024,1024]{2,3,1,0:T(8,128)} %copy.47), kind=kOutput, calls=%fused_computation.4 | convolution fusion | flops 4305451008 | bytes 20979712 | tf_op jit(solution)/shard_map/bnm,bkm->bnk/dot_general | solution.py:70
  182.6 12.6 %multiply_convert_fusion.1 = (bf16[2,1024,1024]{1,2,0:T(8,128)(2,1)}, bf16[2,1024,1024]{1,2,0:T(8,128)(2,1)}) fusion(f32[2,1024,1024]{1,2,0:T(8,128)} %get-tuple-element.34, f32[2]{0:T(128)S(1)} %get-tuple-element.29, f32[1024,1024]{0,1:T(8,128)} %fusion.4, f32[2,1024,1024]{1,2,0:T(8,128)} %get-tuple-element.36, f32[2]{0:T(128)S(1)} %get-tuple-element.30), kind=kLoop, calls=%fused_computation.5 | loop fusion | flops 16777216 | bytes 29360144 | tf_op jit(solution)/shard_map/convert_element_type | solution.py:26
  195.2 10.1 %fusion.25 = bf16[2,512,1024]{2,1,0:T(8,128)(2,1)} fusion(bf16[2,1024,1024]{1,2,0:T(8,128)(2,1)} %get-tuple-element.31, s32[]{:T(128)S(6)} %select_n.2), kind=kOutput, calls=%fused_computation.43 | convolution fusion | flops 4296015872 | bytes 12582916 | tf_op jit(solution)/shard_map/bij,bjk->bik/dot_general | solution.py:18
  205.2 8.7 %fusion.21 = bf16[2,512,1024]{2,1,0:T(8,128)(2,1)S(1)} fusion(bf16[2,1024,1024]{1,2,0:T(8,128)(2,1)} %get-tuple-element.31, bf16[2,512,1024]{2,1,0:T(8,128)(2,1)} %fusion.25), kind=kOutput, calls=%fused_computation.39 | convolution fusion | flops 4296015872 | bytes 8388608 | tf_op jit(solution)/shard_map/bij,bjk->bik/dot_general | solution.py:18
  213.9 7.8 %fusion = f32[2,512,1024]{1,2,0:T(8,128)} fusion(f32[2,1024,1024]{1,2,0:T(8,128)} %get-tuple-element.34, f32[2]{0:T(128)S(1)} %get-tuple-element.29, bf16[2,512,1024]{2,1,0:T(8,128)(2,1)S(1)} %fusion.21), kind=kOutput, calls=%fused_computation.9 | convolution fusion | flops 2151677952 | bytes 14680072 | tf_op jit(solution)/shard_map/bij,bjk->bik/dot_general | solution.py:18
  221.7 12.3 %fusion.17 = f32[2,512,1024]{2,1,0:T(8,128)} fusion(bf16[2,1024,1024]{1,2,0:T(8,128)(2,1)} %get-tuple-element.32, bf16[2,1024,1024]{2,1,0:T(8,128)(2,1)} %copy-done.4, f32[2,512,1024]{1,2,0:T(8,128)} %fusion, bf16[2,1024,1024]{1,2,0:T(8,128)(2,1)} %get-tuple-element.31, s32[]{:T(128)S(6)} %select_n.2), kind=kOutput, calls=%fused_computation.35 | convolution fusion | flops 4301258752 | bytes 18874372 | tf_op jit(solution)/shard_map/bij,bjk->bik/dot_general | solution.py:18
  233.9 5.4 %copy.49 = f32[2,512,1024]{1,2,0:T(8,128)} copy(f32[2,512,1024]{2,1,0:T(8,128)} %fusion.17) | data formatting | bytes 8388608 | tf_op jit(solution)/shard_map/bij,bjk->bik/dot_general | solution.py:18
  239.3 10.6 %fusion.13 = bf16[2,512,1024]{2,1,0:T(8,128)(2,1)} fusion(bf16[2,1024,1024]{1,2,0:T(8,128)(2,1)} %get-tuple-element.32, f32[2,512,1024]{2,1,0:T(8,128)} %fusion.17), kind=kOutput, calls=%fused_computation.31 | convolution fusion | flops 4297064448 | bytes 10485760 | tf_op jit(solution)/shard_map/bij,bjk->bik/dot_general | solution.py:18
  250.0 8.6 %fusion.9 = bf16[2,512,1024]{2,1,0:T(8,128)(2,1)S(1)} fusion(bf16[2,1024,1024]{1,2,0:T(8,128)(2,1)} %get-tuple-element.32, bf16[2,512,1024]{2,1,0:T(8,128)(2,1)} %fusion.13), kind=kOutput, calls=%fused_computation.27 | convolution fusion | flops 4296015872 | bytes 8388608 | tf_op jit(solution)/shard_map/bij,bjk->bik/dot_general | solution.py:18
  258.6 9.0 %subtract_multiply_fusion = f32[2,512,1024]{1,2,0:T(8,128)} fusion(f32[2,512,1024]{1,2,0:T(8,128)} %copy.49, f32[2]{0:T(128)S(1)} %get-tuple-element.28, f32[2,1024,1024]{1,2,0:T(8,128)} %get-tuple-element.36, f32[2]{0:T(128)S(1)} %get-tuple-element.30, bf16[2,512,1024]{2,1,0:T(8,128)(2,1)S(1)} %fusion.9), kind=kOutput, calls=%fused_computation.13 | convolution fusion | flops 2154823680 | bytes 18874384 | tf_op jit(solution)/shard_map/bij,bjk->bik/dot_general | solution.py:18
  267.5 2.8 multiply_reduce_fusion
  270.4 4.9 %psum.7 = f32[2]{0:T(128)S(1)} all-reduce(f32[2]{0:T(128)S(1)} %multiply_reduce_fusion), channel_id=1, replica_groups=mesh['batch'=4,'hidden'=4,'solver'=2] {'solver'}, use_global_device_ids=true, to_apply=%region_6.0 | all-reduce | flops 2 | bytes 16 | tf_op jit(solution)/shard_map/psum | solution.py:93
  275.3 4.8 %broadcast_divide_fusion = f32[2,512,1024]{1,2,0:T(8,128)} fusion(f32[2,512,1024]{1,2,0:T(8,128)} %subtract_multiply_fusion, f32[2]{0:T(128)S(1)} %add_sqrt_fusion), kind=kLoop, calls=%fused_computation.25 | loop fusion | flops 1048576 | bytes 8388616 | tf_op jit(solution)/shard_map/div | solution.py:95
  280.1 5.5 %copy.60 = f32[512,2048]{1,0:T(8,128)} copy(f32[512,2048]{0,1:T(8,128)} %bitcast.62) | data formatting | bytes 8388608
  285.6 3.6 subtract_convert_fusion
  291.7 6.0 %convolution_convert_fusion = bf16[2,1024,4,256]{3,1,2,0:T(8,128)(2,1)} fusion(bf16[512,2,1024,1]{0,2,3,1:T(8,128)(2,1)} %bitcast.66, bf16[4,256,512,1]{2,1,0,3:T(8,128)(2,1)S(1)} %bitcast.70), kind=kOutput, calls=%fused_computation.20 | convolution fusion | flops 2149580800 | bytes 7340032 | tf_op jit(solution)/shard_map/fco,btf->cbot/dot_general | solution.py:53
  300.6 107.4 %reduce-scatter.5.cloned.1.call-done = bf16[1024,256]{1,0:T(8,128)(2,1)} async-done(((bf16[8192,256]{1,0:T(8,128)(2,1)}), bf16[1024,256]{1,0:T(8,128)(2,1)}) %reduce-scatter.5.cloned.1.call-update) | async-done | bytes 524304 | tf_op jit(solution)/shard_map/reduce_scatter | solution.py:57
  409.9 7.8 %constant_dynamic-slice_fusion = (f32[2,512,1024]{1,2,0:T(8,128)}, f32[2,512,1024]{1,2,0:T(8,128)}) fusion(f32[2,1024,1024]{1,2,0:T(8,128)} %get-tuple-element.36, s32[]{:T(128)S(6)} %select_n.2, f32[2,1024,1024]{1,2,0:T(8,128)} %get-tuple-element.34), kind=kLoop, calls=%fused_computation.50 | loop fusion | bytes 16777220 | tf_op jit(solution)/shard_map/dynamic_slice | solution.py:77
  417.7 5.3 %copy.57 = f32[2,512,1024]{2,1,0:T(8,128)} copy(f32[2,512,1024]{1,2,0:T(8,128)} %get-tuple-element.37) | data formatting | bytes 8388608 | tf_op jit(solution)/shard_map/dynamic_slice | solution.py:77
  423.0 5.3 %copy.56 = f32[2,512,1024]{2,1,0:T(8,128)} copy(f32[2,512,1024]{1,2,0:T(8,128)} %get-tuple-element.38) | data formatting | bytes 8388608 | tf_op jit(solution)/shard_map/dynamic_slice | solution.py:76
  428.4 9.2 %collective-permute-done.2 = bf16[1024,256]{1,0:T(8,128)(2,1)S(1)} collective-permute-done((bf16[1024,256]{1,0:T(8,128)(2,1)}, bf16[1024,256]{1,0:T(8,128)(2,1)S(1)}, u32[]{:S(2)}, u32[]{:S(2)}) %collective-permute-start.2) | collective-permute-done | bytes 524320 | tf_op jit(solution)/shard_map/ppermute | solution.py:99
  (32 shorter events, 13.5 us)
Async XLA Ops:
  7.2 20.3 %all-gather.8.cloned.1.call-start = ((), (), s32[]{:S(2)}) async-start(), calls=%async_computation.5 | async-start | bytes 1310720 | tf_op jit(solution)/shard_map/all_gather | solution.py:59
  7.9 112.9 %all-gather.10.cloned.1.call-start = ((), (), s32[]{:S(2)}) async-start(), calls=%async_computation.6 | async-start | bytes 4718592 | tf_op jit(solution)/shard_map/all_gather | solution.py:62
  7.9 16.6 %collective-permute-start = (bf16[1024,256]{1,0:T(8,128)(2,1)}, bf16[1024,256]{1,0:T(8,128)(2,1)S(1)}, u32[]{:S(2)}, u32[]{:S(2)}) collective-permute-start(bf16[1024,256]{1,0:T(8,128)(2,1)} %param.6), channel_id=1, source_target_pairs={{0,0},{8,1},{16,2},{24,3},{1,4},{9,5},{17,6},{25,7},{2,8},{10,9},{... | collective-permute-start | bytes 1572872 | tf_op jit(solution)/shard_map/ppermute | solution.py:61
  24.5 0.8 copy-start.2
  25.4 128.4 %all-gather.6.cloned.1.call-start = ((), (), s32[]{:S(2)}) async-start(), calls=%async_computation.2 | async-start | bytes 3145728 | tf_op jit(solution)/shard_map/all_gather | solution.py:60
  27.5 240.0 %reduce-scatter.3.cloned.1.call-start = ((), (), s32[]{:S(2)}) async-start(), calls=%async_computation.3 | async-start | bytes 4718592 | tf_op jit(solution)/shard_map/reduce_scatter | solution.py:57
  44.9 2.5 copy-start
  44.9 2.9 copy-start.1
  120.8 287.2 %reduce-scatter.5.cloned.1.call-start = ((), (), s32[]{:S(2)}) async-start(), calls=%async_computation.4 | async-start | bytes 4718592 | tf_op jit(solution)/shard_map/reduce_scatter | solution.py:57
  161.2 11.6 %copy-start.4 = (bf16[2,1024,1024]{2,1,0:T(8,128)(2,1)}, bf16[2,1024,1024]{2,1,0:T(8,128)(2,1)S(1)}, u32[]{:S(2)}) copy-start(bf16[2,1024,1024]{2,1,0:T(8,128)(2,1)S(1)} %bitcast_convert_fusion) | copy-start | bytes 12582916
  297.6 1.0 copy-start.3
  298.7 129.7 %collective-permute-start.1 = (bf16[1024,256]{1,0:T(8,128)(2,1)S(1)}, bf16[1024,256]{1,0:T(8,128)(2,1)S(1)}, u32[]{:S(2)}, u32[]{:S(2)}) collective-permute-start(bf16[1024,256]{1,0:T(8,128)(2,1)S(1)} %copy-done.3), channel_id=1, source_target_pairs={{0,0},{1,8},{2,16},{3,24},{4,1},{5,9},{6,17},{7,25},{8,2},{9,10},{... | collective-permute-start | bytes 1572872 | tf_op jit(solution)/shard_map/ppermute | solution.py:92
  408.0 29.6 %collective-permute-start.2 = (bf16[1024,256]{1,0:T(8,128)(2,1)}, bf16[1024,256]{1,0:T(8,128)(2,1)S(1)}, u32[]{:S(2)}, u32[]{:S(2)}) collective-permute-start(bf16[1024,256]{1,0:T(8,128)(2,1)} %reduce-scatter.5.cloned.1.call-done), channel_id=1, source_target_pairs={{0,0},{1,8},{2,16},{3,24},{4,1},{5,9},{6,17},{7,25},{8,2},{9,10},{... | collective-permute-start | bytes 1572872 | tf_op jit(solution)/shard_map/ppermute | solution.py:99
Sparse Core Ops, SparseCore 0:
  9.5 17.8 all-gather.7
  30.2 90.5 all-gather.9
  122.3 31.4 all-gather.5
  157.8 89.4 reduce-scatter.2
  297.8 110.1 reduce-scatter.4

commit v2 on v1

--- a/solution.py
+++ b/solution.py
@@ -34,7 +34,7 @@
     return (5.0 * start.astype(jnp.float32) - power) * 0.25
 
 
-def body(activations, cotangent, weight, left_old, right_old, *, n_batch, n_feat):
+def body(activations, cotangent, weight, left_old, right_old, *, n_batch, n_solver, n_feat):
     rows_here = weight.shape[0]
     nblocks = weight.shape[1] // BLOCK
     per_batch = n_feat // n_batch
@@ -57,7 +57,15 @@
         return lax.psum_scatter(partial, FEATURES, scatter_dimension=0, tiled=True)
 
     acts_all = lax.all_gather(activations, "batch", axis=0, tiled=False)
-    acts_block = lax.all_gather(acts_all, "solver", axis=2, tiled=True)
+    here = lax.axis_index("solver")
+    acts_block = jnp.zeros((n_batch, tokens, n_solver * rows_here), acts_all.dtype)
+    for shift in range(n_solver):
+        part = acts_all
+        if shift > 0:
+            pairs = [(at, (at + shift) % n_solver) for at in range(n_solver)]
+            part = lax.ppermute(acts_all, "solver", pairs)
+        first_col = lax.rem(here + n_solver - shift, n_solver) * rows_here
+        acts_block = lax.dynamic_update_slice_in_dim(acts_block, part, first_col, 2)
     cot_moved = lax.ppermute(cotangent, ALL, from_owner)
     cot_all = lax.all_gather(cot_moved, FEATURES, axis=0, tiled=False)
     cot_all = cot_all.reshape(per_batch, n_batch, out_rows, tokens)
@@ -96,6 +104,7 @@
     direction = jnp.transpose(scaled_update, (1, 0, 2)).reshape(rows_here, nblocks * BLOCK)
     new_weight = (weight.astype(jnp.float32) - LEARN_RATE * direction).astype(jnp.bfloat16)
     second_sum = reduce_forward(partial_forward(new_weight))
+    second_sum, new_left, new_right = lax.optimization_barrier((second_sum, new_left, new_right))
     second_out = lax.ppermute(second_sum, ALL, to_owner)
     return (first_out, new_left, new_right, direction, second_out)
 
@@ -120,7 +129,14 @@
 
     def step(activations, cotangent, weight, left_old, right_old):
         return body(
-            activations, cotangent, weight, left_old, right_old, n_batch=n_batch, n_feat=n_feat
+            activations,
+            cotangent,
+            weight,
+            left_old,
+            right_old,
+            n_batch=n_batch,
+            n_solver=mesh.shape["solver"],
+            n_feat=n_feat,
         )
 
     return jax.shard_map(step, mesh=mesh, in_specs=in_specs, out_specs=out_specs, check_vma=False)

time: 450 us -> 420 us (0.933)
  waiting for transfers between devices: 227 us -> 180 us
  starting transfers between devices: 8.62 us -> 24.4 us
    all_gather x1 -> x0, waiting for transfers between devices: 32.8 us -> none  [body(): acts_block = lax.all_gather(acts_all, 'solver', axis=2, tiled=True)]
    ppermute x1, waiting for transfers between devices: 9.22 us -> 27.6 us  [body(): second_out = lax.ppermute(second_sum, ALL, to_owner)]
    reduce_scatter x2, waiting for transfers between devices: 107 us -> 89.5 us  [reduce_forward(): return lax.psum_scatter(partial, FEATURES, scatter_dimension=0, tiled=True)]
    ppermute x0 -> x1, starting transfers between devices: none -> 15.8 us  [body(): part = lax.ppermute(acts_all, 'solver', pairs)]
    all_gather x1, waiting for transfers between devices: 62.3 us -> 47.6 us  [body(): cot_all = lax.all_gather(cot_moved, FEATURES, axis=0, tiled=False)]
    unnamed x15 -> x14, local copies, waits for them, and re-layouts: 26.6 us -> 20.2 us
    reshape x0 -> x1, local copies, waits for them, and re-layouts: none -> 5.49 us  [body(): jnp.transpose(scaled_update, (1, 0, 2)).reshape(rows_here, nblocks * BLOCK)]
  transfers between devices with their start and end apart: 8 -> 8, of which waited for: 6 -> 5; matrix products, arithmetic and copies ran while one was open for 36% -> 40% of each run, Pallas kernels for 0% -> 0%
where the time goes in v2:
time: 420 us; the launch traced here: 415 us
  waiting for transfers between devices  180 us (43%)
  matrix products  106 us (25%)
  local copies, waits for them, and re-layouts  60.3 us (14%)
  other arithmetic  26.2 us (6%)
  starting transfers between devices  24.4 us (6%)
  between operations  14.1 us (3%)
  blocking collectives  4.92 us (1%)
    reduce_scatter x2, waiting for transfers between devices, reduce_forward(): return lax.psum_scatter(partial, FEATURES, scatter_dimension=0, tiled=True)  89.5 us
    dot_general x7, matrix products, product(): jnp.einsum('bij,bjk->bik', left_mat, right_mat, preferred_element_type=jn...  67.3 us
    all_gather x1, waiting for transfers between devices, body(): cot_all = lax.all_gather(cot_moved, FEATURES, axis=0, tiled=False)  47.6 us
    ppermute x1, waiting for transfers between devices, body(): second_out = lax.ppermute(second_sum, ALL, to_owner)  27.6 us
    unnamed x14, local copies, waits for them, and re-layouts  20.2 us
    ppermute x1, starting transfers between devices, body(): part = lax.ppermute(acts_all, 'solver', pairs)  15.8 us
    dynamic_slice x2, local copies, waits for them, and re-layouts, body(): lax.dynamic_slice_in_dim(right_all, first_row, rows_here, 1)[None]  13.1 us
    convert_element_type x1, other arithmetic, prepare(): newton_step.astype(jnp.bfloat16)  12.2 us
  transfers between devices with their start and end apart: 8, of which 5 were waited for; matrix products, arithmetic and copies ran while one was open for 40% of the time, Pallas kernels for 0%

profile of v2, /device:TPU:4, one launch (start us, length us, event | category | flops | bytes accessed | tf_op | source)
XLA Modules:
  0.0 415.2 jit_solution(4227732098720041947)
XLA Ops:
  7.9 4.4 %collective-permute-start = (bf16[1024,256]{1,0:T(8,128)(2,1)}, bf16[1024,256]{1,0:T(8,128)(2,1)S(1)}, u32[]{:S(2)}, u32[]{:S(2)}) collective-permute-start(bf16[1024,256]{1,0:T(8,128)(2,1)} %param.6), channel_id=1, source_target_pairs={{0,0},{8,1},{16,2},{24,3},{1,4},{9,5},{17,6},{25,7},{2,8},{10,9},{... | collective-permute-start | bytes 1572872 | tf_op jit(solution)/shard_map/ppermute | solution.py:69
  12.4 12.1 %collective-permute-done = bf16[1024,256]{1,0:T(8,128)(2,1)S(1)} collective-permute-done((bf16[1024,256]{1,0:T(8,128)(2,1)}, bf16[1024,256]{1,0:T(8,128)(2,1)S(1)}, u32[]{:S(2)}, u32[]{:S(2)}) %collective-permute-start) | collective-permute-done | bytes 524320 | tf_op jit(solution)/shard_map/ppermute | solution.py:69
  27.5 15.8 %collective-permute-start.1 = (bf16[4,256,512]{2,1,0:T(8,128)(2,1)}, bf16[4,256,512]{2,1,0:T(8,128)(2,1)}, u32[]{:S(2)}, u32[]{:S(2)}) collective-permute-start(bf16[4,256,512]{2,1,0:T(8,128)(2,1)} %bitcast.68), channel_id=1, source_target_pairs={{0,1},{1,0},{2,3},{3,2},{4,5},{5,4},{6,7},{7,6},{8,9},{9,8},{10,11... | collective-permute-start | bytes 3145736 | tf_op jit(solution)/shard_map/ppermute | solution.py:66
  43.2 8.7 %copy.35 = f32[1,2,1024,1024]{2,3,1,0:T(8,128)} copy(f32[1,2,1024,1024]{3,2,1,0:T(8,128)} %param.8) | data formatting | bytes 16777216 | tf_op args[3]
  51.9 8.8 %copy.47 = f32[1,2,1024,1024]{2,3,1,0:T(8,128)} copy(f32[1,2,1024,1024]{3,2,1,0:T(8,128)} %param.9) | data formatting | bytes 16777216 | tf_op args[4]
  60.7 2.5 fusion.4
  63.6 4.4 %convert_bitcast_fusion = bf16[2,4,1024,256]{2,3,0,1:T(8,128)(2,1)} fusion(bf16[4,256,512,1]{2,1,3,0:T(8,128)(2,1)S(1)} %bitcast.69, bf16[64,2,8,1024]{3,2,1,0:T(8,128)(2,1)S(1)} %bitcast.67), kind=kOutput, calls=%fused_computation.17 | convolution fusion | flops 2149580800 | bytes 7340032 | tf_op jit(solution)/shard_map/fco,btf->cbot/dot_general | solution.py:53
  68.0 6.3 %copy.37 = bf16[2,4,1024,256]{3,2,1,0:T(8,128)(2,1)} copy(bf16[2,4,1024,256]{2,3,0,1:T(8,128)(2,1)} %convert_bitcast_fusion) | data formatting | bytes 8388608 | tf_op jit(solution)/shard_map/convert_element_type | solution.py:54
  76.1 47.6 %all-gather.7.cloned.1.call-done = bf16[8192,256]{1,0:T(8,128)(2,1)} async-done(((bf16[1024,256]{1,0:T(8,128)(2,1)}), bf16[8192,256]{1,0:T(8,128)(2,1)}) %all-gather.7.cloned.1.call-update) | async-done | bytes 4194320 | tf_op jit(solution)/shard_map/all_gather | solution.py:70
  124.0 6.9 %bitcast_convert_fusion = bf16[2,1024,1024]{2,1,0:T(8,128)(2,1)S(1)} fusion(bf16[2,4,1024,256]{3,2,1,0:T(8,128)(2,1)} %bitcast.72, bf16[4,256,1024]{2,1,0:T(8,128)(2,1)S(1)} %constant_dynamic-update-slice_fusion), kind=kOutput, calls=%fused_computation.1 | convolution fusion | flops 4297064448 | bytes 10485760 | tf_op jit(solution)/shard_map/cbot,btf->cof/dot_general | solution.py:75
  130.9 11.6 %abs_reduce_fusion.1 = (f32[2,1024]{1,0:T(2,128)S(1)}, f32[2,1024,1024]{1,2,0:T(8,128)}) fusion(bf16[2,1024,1024]{2,1,0:T(8,128)(2,1)S(1)} %bitcast_convert_fusion, f32[1,2,1024,1024]{2,3,1,0:T(8,128)} %copy.35), kind=kOutput, calls=%fused_computation.6 | convolution fusion | flops 4305451008 | bytes 20979712 | tf_op jit(solution)/shard_map/bnm,bnk->bmk/dot_general | solution.py:77
  142.5 9.5 %abs_reduce_fusion = (f32[2,1024]{1,0:T(2,128)S(1)}, f32[2,1024,1024]{1,2,0:T(8,128)}) fusion(bf16[2,1024,1024]{2,1,0:T(8,128)(2,1)S(1)} %bitcast_convert_fusion, f32[1,2,1024,1024]{2,3,1,0:T(8,128)} %copy.47), kind=kOutput, calls=%fused_computation.4 | convolution fusion | flops 4305451008 | bytes 20979712 | tf_op jit(solution)/shard_map/bnm,bkm->bnk/dot_general | solution.py:78
  152.3 12.2 %multiply_convert_fusion.1 = (bf16[2,1024,1024]{1,2,0:T(8,128)(2,1)}, bf16[2,1024,1024]{1,2,0:T(8,128)(2,1)}) fusion(f32[2,1024,1024]{1,2,0:T(8,128)} %get-tuple-element.40, f32[2]{0:T(128)S(1)} %get-tuple-element.35, f32[1024,1024]{0,1:T(8,128)} %fusion.4, f32[2,1024,1024]{1,2,0:T(8,128)} %get-tuple-element.42, f32[2]{0:T(128)S(1)} %get-tuple-element.36), kind=kLoop, calls=%fused_computation.5 | loop fusion | flops 16777216 | bytes 29360144 | tf_op jit(solution)/shard_map/convert_element_type | solution.py:26
  164.5 10.1 %fusion.25 = bf16[2,512,1024]{2,1,0:T(8,128)(2,1)} fusion(bf16[2,1024,1024]{1,2,0:T(8,128)(2,1)} %get-tuple-element.37, s32[]{:T(128)S(6)} %select_n.13), kind=kOutput, calls=%fused_computation.43 | convolution fusion | flops 4296015872 | bytes 12582916 | tf_op jit(solution)/shard_map/bij,bjk->bik/dot_general | solution.py:18
  174.6 8.7 %fusion.21 = bf16[2,512,1024]{2,1,0:T(8,128)(2,1)S(1)} fusion(bf16[2,1024,1024]{1,2,0:T(8,128)(2,1)} %get-tuple-element.37, bf16[2,512,1024]{2,1,0:T(8,128)(2,1)} %fusion.25), kind=kOutput, calls=%fused_computation.39 | convolution fusion | flops 4296015872 | bytes 8388608 | tf_op jit(solution)/shard_map/bij,bjk->bik/dot_general | solution.py:18
  183.3 7.8 %fusion = f32[2,512,1024]{1,2,0:T(8,128)} fusion(f32[2,1024,1024]{1,2,0:T(8,128)} %get-tuple-element.40, f32[2]{0:T(128)S(1)} %get-tuple-element.35, bf16[2,512,1024]{2,1,0:T(8,128)(2,1)S(1)} %fusion.21), kind=kOutput, calls=%fused_computation.9 | convolution fusion | flops 2151677952 | bytes 14680072 | tf_op jit(solution)/shard_map/bij,bjk->bik/dot_general | solution.py:18
  191.1 12.6 %fusion.17 = f32[2,512,1024]{2,1,0:T(8,128)} fusion(bf16[2,1024,1024]{1,2,0:T(8,128)(2,1)} %get-tuple-element.38, bf16[2,1024,1024]{2,1,0:T(8,128)(2,1)} %copy-done.4, f32[2,512,1024]{1,2,0:T(8,128)} %fusion, bf16[2,1024,1024]{1,2,0:T(8,128)(2,1)} %get-tuple-element.37, s32[]{:T(128)S(6)} %select_n.13), kind=kOutput, calls=%fused_computation.35 | convolution fusion | flops 4301258752 | bytes 18874372 | tf_op jit(solution)/shard_map/bij,bjk->bik/dot_general | solution.py:18
  203.7 5.4 %copy.49 = f32[2,512,1024]{1,2,0:T(8,128)} copy(f32[2,512,1024]{2,1,0:T(8,128)} %fusion.17) | data formatting | bytes 8388608 | tf_op jit(solution)/shard_map/bij,bjk->bik/dot_general | solution.py:18
  209.1 10.6 %fusion.13 = bf16[2,512,1024]{2,1,0:T(8,128)(2,1)} fusion(bf16[2,1024,1024]{1,2,0:T(8,128)(2,1)} %get-tuple-element.38, f32[2,512,1024]{2,1,0:T(8,128)} %fusion.17), kind=kOutput, calls=%fused_computation.31 | convolution fusion | flops 4297064448 | bytes 10485760 | tf_op jit(solution)/shard_map/bij,bjk->bik/dot_general | solution.py:18
  219.7 8.6 %fusion.9 = bf16[2,512,1024]{2,1,0:T(8,128)(2,1)S(1)} fusion(bf16[2,1024,1024]{1,2,0:T(8,128)(2,1)} %get-tuple-element.38, bf16[2,512,1024]{2,1,0:T(8,128)(2,1)} %fusion.13), kind=kOutput, calls=%fused_computation.27 | convolution fusion | flops 4296015872 | bytes 8388608 | tf_op jit(solution)/shard_map/bij,bjk->bik/dot_general | solution.py:18
  228.3 9.0 %subtract_multiply_fusion = f32[2,512,1024]{1,2,0:T(8,128)} fusion(f32[2,512,1024]{1,2,0:T(8,128)} %copy.49, f32[2]{0:T(128)S(1)} %get-tuple-element.34, f32[2,1024,1024]{1,2,0:T(8,128)} %get-tuple-element.42, f32[2]{0:T(128)S(1)} %get-tuple-element.36, bf16[2,512,1024]{2,1,0:T(8,128)(2,1)S(1)} %fusion.9), kind=kOutput, calls=%fused_computation.13 | convolution fusion | flops 2154823680 | bytes 18874384 | tf_op jit(solution)/shard_map/bij,bjk->bik/dot_general | solution.py:18
  237.3 2.8 multiply_reduce_fusion
  240.1 4.9 %psum.7 = f32[2]{0:T(128)S(1)} all-reduce(f32[2]{0:T(128)S(1)} %multiply_reduce_fusion), channel_id=1, replica_groups=mesh['batch'=4,'hidden'=4,'solver'=2] {'solver'}, use_global_device_ids=true, to_apply=%region_6.0 | all-reduce | flops 2 | bytes 16 | tf_op jit(solution)/shard_map/psum | solution.py:101
  245.1 4.8 %broadcast_divide_fusion = f32[2,512,1024]{1,2,0:T(8,128)} fusion(f32[2,512,1024]{1,2,0:T(8,128)} %subtract_multiply_fusion, f32[2]{0:T(128)S(1)} %add_sqrt_fusion), kind=kLoop, calls=%fused_computation.25 | loop fusion | flops 1048576 | bytes 8388616 | tf_op jit(solution)/shard_map/div | solution.py:103
  249.9 5.5 %copy.56 = f32[512,2048]{1,0:T(8,128)} copy(f32[512,2048]{0,1:T(8,128)} %bitcast.62) | data formatting | bytes 8388608 | tf_op jit(solution)/shard_map/reshape | solution.py:104
  255.3 3.6 subtract_convert_fusion
  261.4 5.9 %convolution_convert_fusion = bf16[2,1024,4,256]{3,1,2,0:T(8,128)(2,1)} fusion(bf16[512,2,1024,1]{0,2,3,1:T(8,128)(2,1)} %bitcast.66, bf16[4,256,512,1]{2,1,0,3:T(8,128)(2,1)S(1)} %bitcast.71), kind=kOutput, calls=%fused_computation.20 | convolution fusion | flops 2149580800 | bytes 7340032 | tf_op jit(solution)/shard_map/fco,btf->cbot/dot_general | solution.py:53
  267.3 7.8 %constant_dynamic-slice_fusion = (f32[2,512,1024]{1,2,0:T(8,128)}, f32[2,512,1024]{1,2,0:T(8,128)}) fusion(f32[2,1024,1024]{1,2,0:T(8,128)} %get-tuple-element.42, s32[]{:T(128)S(6)} %select_n.13, f32[2,1024,1024]{1,2,0:T(8,128)} %get-tuple-element.40), kind=kLoop, calls=%fused_computation.50 | loop fusion | bytes 16777220 | tf_op jit(solution)/shard_map/dynamic_slice | solution.py:85
  275.2 5.3 %copy.59 = f32[2,512,1024]{2,1,0:T(8,128)} copy(f32[2,512,1024]{1,2,0:T(8,128)} %get-tuple-element.43) | data formatting | bytes 8388608 | tf_op jit(solution)/shard_map/dynamic_slice | solution.py:85
  280.5 5.4 %copy.58 = f32[2,512,1024]{2,1,0:T(8,128)} copy(f32[2,512,1024]{1,2,0:T(8,128)} %get-tuple-element.44) | data formatting | bytes 8388608 | tf_op jit(solution)/shard_map/dynamic_slice | solution.py:84
  287.8 89.5 %reduce-scatter.5.cloned.1.call-done = bf16[1024,256]{1,0:T(8,128)(2,1)} async-done(((bf16[8192,256]{1,0:T(8,128)(2,1)}), bf16[1024,256]{1,0:T(8,128)(2,1)}) %reduce-scatter.5.cloned.1.call-update) | async-done | bytes 524304 | tf_op jit(solution)/shard_map/reduce_scatter | solution.py:57
  379.3 27.6 %collective-permute-done.3 = bf16[1024,256]{1,0:T(8,128)(2,1)S(1)} collective-permute-done((bf16[1024,256]{1,0:T(8,128)(2,1)}, bf16[1024,256]{1,0:T(8,128)(2,1)S(1)}, u32[]{:S(2)}, u32[]{:S(2)}) %collective-permute-start.3) | collective-permute-done | bytes 524320 | tf_op jit(solution)/shard_map/ppermute | solution.py:108
  (34 shorter events, 14.3 us)
Async XLA Ops:
  7.2 20.3 %all-gather.5.cloned.1.call-start = ((), (), s32[]{:S(2)}) async-start(), calls=%async_computation.4 | async-start | bytes 1310720 | tf_op jit(solution)/shard_map/all_gather | solution.py:59
  7.9 115.8 %all-gather.7.cloned.1.call-start = ((), (), s32[]{:S(2)}) async-start(), calls=%async_computation.5 | async-start | bytes 4718592 | tf_op jit(solution)/shard_map/all_gather | solution.py:70
  7.9 16.6 %collective-permute-start = (bf16[1024,256]{1,0:T(8,128)(2,1)}, bf16[1024,256]{1,0:T(8,128)(2,1)S(1)}, u32[]{:S(2)}, u32[]{:S(2)}) collective-permute-start(bf16[1024,256]{1,0:T(8,128)(2,1)} %param.6), channel_id=1, source_target_pairs={{0,0},{8,1},{16,2},{24,3},{1,4},{9,5},{17,6},{25,7},{2,8},{10,9},{... | collective-permute-start | bytes 1572872 | tf_op jit(solution)/shard_map/ppermute | solution.py:69
  24.5 0.8 copy-start.2
  25.4 211.9 %reduce-scatter.3.cloned.1.call-start = ((), (), s32[]{:S(2)}) async-start(), calls=%async_computation.2 | async-start | bytes 4718592 | tf_op jit(solution)/shard_map/reduce_scatter | solution.py:57
  27.5 47.2 %collective-permute-start.1 = (bf16[4,256,512]{2,1,0:T(8,128)(2,1)}, bf16[4,256,512]{2,1,0:T(8,128)(2,1)}, u32[]{:S(2)}, u32[]{:S(2)}) collective-permute-start(bf16[4,256,512]{2,1,0:T(8,128)(2,1)} %bitcast.68), channel_id=1, source_target_pairs={{0,1},{1,0},{2,3},{3,2},{4,5},{5,4},{6,7},{7,6},{8,9},{9,8},{10,11... | collective-permute-start | bytes 3145736 | tf_op jit(solution)/shard_map/ppermute | solution.py:66
  60.7 2.5 copy-start
  60.7 2.9 copy-start.1
  123.7 253.6 %reduce-scatter.5.cloned.1.call-start = ((), (), s32[]{:S(2)}) async-start(), calls=%async_computation.3 | async-start | bytes 4718592 | tf_op jit(solution)/shard_map/reduce_scatter | solution.py:57
  130.9 11.6 %copy-start.4 = (bf16[2,1024,1024]{2,1,0:T(8,128)(2,1)}, bf16[2,1024,1024]{2,1,0:T(8,128)(2,1)S(1)}, u32[]{:S(2)}) copy-start(bf16[2,1024,1024]{2,1,0:T(8,128)(2,1)S(1)} %bitcast_convert_fusion) | copy-start | bytes 12582916
  280.5 5.4 %copy-start.3 = (bf16[1024,256]{1,0:T(8,128)(2,1)S(1)}, bf16[1024,256]{1,0:T(8,128)(2,1)}, u32[]{:S(2)}) copy-start(bf16[1024,256]{1,0:T(8,128)(2,1)} %reduce-scatter.3.cloned.1.call-done) | copy-start | bytes 1572868
  285.9 93.4 %collective-permute-start.2 = (bf16[1024,256]{1,0:T(8,128)(2,1)S(1)}, bf16[1024,256]{1,0:T(8,128)(2,1)S(1)}, u32[]{:S(2)}, u32[]{:S(2)}) collective-permute-start(bf16[1024,256]{1,0:T(8,128)(2,1)S(1)} %copy-done.3), channel_id=1, source_target_pairs={{0,0},{1,8},{2,16},{3,24},{4,1},{5,9},{6,17},{7,25},{8,2},{9,10},{... | collective-permute-start | bytes 1572872 | tf_op jit(solution)/shard_map/ppermute | solution.py:100
  377.4 29.6 %collective-permute-start.3 = (bf16[1024,256]{1,0:T(8,128)(2,1)}, bf16[1024,256]{1,0:T(8,128)(2,1)S(1)}, u32[]{:S(2)}, u32[]{:S(2)}) collective-permute-start(bf16[1024,256]{1,0:T(8,128)(2,1)} %reduce-scatter.5.cloned.1.call-done), channel_id=1, source_target_pairs={{0,0},{1,8},{2,16},{3,24},{4,1},{5,9},{6,17},{7,25},{8,2},{9,10},{... | collective-permute-start | bytes 1572872 | tf_op jit(solution)/shard_map/ppermute | solution.py:108
Sparse Core Ops, SparseCore 0:
  9.5 17.8 all-gather.4
  30.2 93.5 all-gather.6
  127.9 87.7 reduce-scatter.2
  267.5 109.8 reduce-scatter.4
